TPU v7x, 32 devices: a whole 2x2x4 slice. The times are simulated.
32 devices in a mesh: ctx: 8 (over z, x), fsdp: 4 (over y, core).
Axes of the slice: x: 2, y: 2, z: 4, core: 2. Of those that a mesh axis runs over, the one named last changes fastest.
Arguments:
- inputs: bfloat16 [8, 512, 1024], P('fsdp', 'ctx'), may hold values from -6 to 6
- gain_one: bfloat16 [1024], P('fsdp'), may hold values from 0.25 to 1.75
- w_qkv: bfloat16 [1024, 3072], P('fsdp')
- w_attn: bfloat16 [1024, 1024], P('fsdp'), may hold values from -0.75 to 0.75
- gain_two: bfloat16 [1024], P('fsdp'), may hold values from 0.25 to 1.75
- w_in: bfloat16 [1024, 5248], P('fsdp'), may hold values from -0.1875 to 0.1875
- w_ffn: bfloat16 [2624, 1024], P('fsdp'), may hold values from -0.125 to 0.125
- cotangent: bfloat16 [8, 512, 1024], P('fsdp', 'ctx'), may hold values from -6 to 6
Outputs:
- output: bfloat16 [8, 512, 1024], P('fsdp', 'ctx')
- grad_input: float32 [8, 512, 1024], P('fsdp', 'ctx')
- grad_gain_one: float32 [1024], P('fsdp')
- grad_w_qkv: float32 [1024, 3072], P('fsdp')
- grad_w_attn: float32 [1024, 1024], P('fsdp')
- grad_gain_two: float32 [1024], P('fsdp')
- grad_w_in: float32 [1024, 5248], P('fsdp')
- grad_w_ffn: float32 [2624, 1024], P('fsdp')
All inputs are finite; a program needn't handle non-finite values.
Results may differ from a plain program's by a relative error of at most 0.023.
Values may be sent and summed in bfloat16 or wider, within the bound.
A program may use at most 256 MiB of HBM per device.

v0:
```python
import math
import jax
import jax.numpy as jnp
from jax import lax
from jax.sharding import PartitionSpec as P

D = 1024
HEADS = 16
HEAD_DIM = 64
FF = 2624
EPSILON = 1e-05
ROPE_THETA = 160000.0


def norm_parts(values_in):
    mean_val = jnp.mean(values_in, axis=-1, keepdims=True)
    centred = values_in - mean_val
    variance = jnp.mean(centred * centred, axis=-1, keepdims=True)
    inv_std = lax.rsqrt(variance + EPSILON)
    return (centred * inv_std, inv_std)


def norm_back(grad_normed, normed, inv_std):
    return inv_std * (
        grad_normed
        - jnp.mean(grad_normed, axis=-1, keepdims=True)
        - normed * jnp.mean(grad_normed * normed, axis=-1, keepdims=True)
    )


def rotary_tables(positions):
    half_dim = HEAD_DIM // 2
    inv_freq = ROPE_THETA ** (-(jnp.arange(half_dim, dtype=jnp.float32) * 2.0) / HEAD_DIM)
    angles = positions.astype(jnp.float32)[:, None] * inv_freq[None, :]
    cosine = jnp.concatenate([jnp.cos(angles), jnp.cos(angles)], axis=-1)[:, None, :]
    sine_part = jnp.concatenate([jnp.sin(angles), jnp.sin(angles)], axis=-1)[:, None, :]
    return (cosine, sine_part)


def rotate(values_in, cosine, sine_part):
    half_dim = values_in.shape[-1] // 2
    turned = jnp.concatenate([-values_in[..., half_dim:], values_in[..., :half_dim]], axis=-1)
    return values_in * cosine + turned * sine_part


def rotate_back(grads, cosine, sine_part):
    half_dim = grads.shape[-1] // 2
    scaled = grads * sine_part
    turned = jnp.concatenate([scaled[..., half_dim:], -scaled[..., :half_dim]], axis=-1)
    return grads * cosine + turned


def gelu_slope(inner_part):
    cumulative = 0.5 * (1.0 + jax.scipy.special.erf(inner_part * 0.7071067811865476))
    density = jnp.exp(-0.5 * inner_part * inner_part) * 0.3989422804014327
    return cumulative + inner_part * density


def attend_piece(state_in, queries, key_piece, value_piece, scale_factor):
    row_max, row_sum, weighted = state_in
    scores = (
        jnp.einsum("bthd,bshd->bths", queries, key_piece, preferred_element_type=jnp.float32)
        * scale_factor
    )
    new_max = jnp.maximum(row_max, jnp.max(scores, axis=-1))
    rescale = jnp.exp(row_max - new_max)
    exp_vals = jnp.exp(scores - new_max[..., None])
    row_sum = row_sum * rescale + jnp.sum(exp_vals, axis=-1)
    weighted = weighted * rescale[..., None] + jnp.einsum(
        "bths,bshd->bthd",
        exp_vals.astype(jnp.bfloat16),
        value_piece,
        preferred_element_type=jnp.float32,
    )
    return (new_max, row_sum, weighted)


def back_piece(queries, grad_mixed, log_sum, row_delta, key_piece, value_piece, scale_factor):
    scores = (
        jnp.einsum("bthd,bshd->bths", queries, key_piece, preferred_element_type=jnp.float32)
        * scale_factor
    )
    probs = jnp.exp(scores - log_sum[..., None])
    grad_values = jnp.einsum(
        "bths,bthd->bshd",
        probs.astype(jnp.bfloat16),
        grad_mixed,
        preferred_element_type=jnp.float32,
    )
    grad_probs = jnp.einsum(
        "bthd,bshd->bths", grad_mixed, value_piece, preferred_element_type=jnp.float32
    )
    grad_scores = (probs * (grad_probs - row_delta[..., None])).astype(jnp.bfloat16)
    grad_query = (
        jnp.einsum("bths,bshd->bthd", grad_scores, key_piece, preferred_element_type=jnp.float32)
        * scale_factor
    )
    grad_keys = (
        jnp.einsum("bths,bthd->bshd", grad_scores, queries, preferred_element_type=jnp.float32)
        * scale_factor
    )
    return (grad_query, grad_keys, grad_values)


def add_at(whole_grads, piece_grads, offset):
    old_part = lax.dynamic_slice_in_dim(whole_grads, offset, piece_grads.shape[1], 1)
    return lax.dynamic_update_slice_in_dim(whole_grads, old_part + piece_grads, offset, 1)


def on_device(inputs, gain_one, w_qkv, w_attn, gain_two, w_in, w_ffn, cotangent):
    seq_dev = inputs.shape[0]
    tok_seq = inputs.shape[1]
    row_count = seq_dev * tok_seq
    seq_len = tok_seq * lax.axis_size("ctx")
    tokens_f = inputs.reshape(row_count, D).astype(jnp.float32)
    grad_out = cotangent.reshape(row_count, D)
    scale_factor = HEAD_DIM ** (-0.5)
    block_len = math.gcd(seq_len, 512)
    blocks_num = seq_len // block_len
    gathered = (
        lax.all_gather(gain_one, "fsdp", axis=0, tiled=True),
        lax.all_gather(w_qkv, "fsdp", axis=0, tiled=True),
        lax.all_gather(w_attn, "fsdp", axis=0, tiled=True),
        lax.all_gather(gain_two, "fsdp", axis=0, tiled=True),
        lax.all_gather(w_in, "fsdp", axis=0, tiled=True),
        lax.all_gather(w_ffn, "fsdp", axis=0, tiled=True),
    )
    full_g1, full_qkv, full_attn, full_g2, full_in, full_ffn = gathered
    normed_one, inv_one = norm_parts(tokens_f)
    input_one = (normed_one * full_g1.astype(jnp.float32)).astype(jnp.bfloat16)
    project = jnp.dot(input_one, full_qkv, preferred_element_type=jnp.float32)
    positions = lax.axis_index("ctx") * tok_seq + jnp.arange(tok_seq, dtype=jnp.int32)
    cosine, sine_part = rotary_tables(positions)
    shaped = project.reshape(seq_dev, tok_seq, 3, HEADS, HEAD_DIM)
    queries = rotate(shaped[:, :, 0], cosine, sine_part).astype(jnp.bfloat16)
    key_rows = rotate(shaped[:, :, 1], cosine, sine_part).astype(jnp.bfloat16)
    value_rows = shaped[:, :, 2].astype(jnp.bfloat16)
    start_state = (
        jnp.full((seq_dev, tok_seq, HEADS), -jnp.inf, jnp.float32),
        jnp.zeros((seq_dev, tok_seq, HEADS), jnp.float32),
        jnp.zeros((seq_dev, tok_seq, HEADS, HEAD_DIM), jnp.float32),
    )
    whole_keys, whole_values = (
        lax.all_gather(key_rows, "ctx", axis=1, tiled=True),
        lax.all_gather(value_rows, "ctx", axis=1, tiled=True),
    )

    def forward_step(state_in, block_index):
        begin = block_index * block_len
        key_piece = lax.dynamic_slice_in_dim(whole_keys, begin, block_len, 1)
        value_piece = lax.dynamic_slice_in_dim(whole_values, begin, block_len, 1)
        return (attend_piece(state_in, queries, key_piece, value_piece, scale_factor), None)

    state_out, unused = lax.scan(forward_step, start_state, jnp.arange(blocks_num, dtype=jnp.int32))
    row_max, row_sum, weighted = state_out
    attn_f = weighted / row_sum[..., None]
    log_sum = row_max + jnp.log(row_sum)
    attn_b = attn_f.reshape(row_count, D).astype(jnp.bfloat16)
    resid = tokens_f + jnp.dot(attn_b, full_attn, preferred_element_type=jnp.float32)
    normed_two, inv_two = norm_parts(resid)
    input_two = (normed_two * full_g2.astype(jnp.float32)).astype(jnp.bfloat16)
    widened = jnp.dot(input_two, full_in, preferred_element_type=jnp.float32)
    inner_part = widened[:, :FF]
    gating = widened[:, FF:]
    activated = jax.nn.gelu(inner_part, approximate=False)
    hidden = (activated * gating).astype(jnp.bfloat16)
    output = (resid + jnp.dot(hidden, full_ffn, preferred_element_type=jnp.float32)).astype(
        jnp.bfloat16
    )
    back_g1, back_qkv, back_attn, back_g2, back_in, back_ffn = gathered
    grad_ffn = jnp.dot(hidden.T, grad_out, preferred_element_type=jnp.float32)
    grad_hidden = jnp.dot(grad_out, back_ffn.T, preferred_element_type=jnp.float32)
    grad_inner = grad_hidden * gating * gelu_slope(inner_part)
    grad_gating = grad_hidden * activated
    grad_wide = jnp.concatenate([grad_inner, grad_gating], axis=-1).astype(jnp.bfloat16)
    grad_in = jnp.dot(input_two.T, grad_wide, preferred_element_type=jnp.float32)
    grad_normed_two = jnp.dot(grad_wide, back_in.T, preferred_element_type=jnp.float32)
    grad_g2 = jnp.sum(grad_normed_two * normed_two, axis=0)
    grad_resid = grad_out.astype(jnp.float32) + norm_back(
        grad_normed_two * back_g2.astype(jnp.float32), normed_two, inv_two
    )
    part_g2, part_in, part_ffn = (
        lax.psum_scatter(
            grad_g2.astype(jnp.bfloat16), "fsdp", scatter_dimension=0, tiled=True
        ).astype(jnp.float32),
        lax.psum_scatter(
            grad_in.astype(jnp.bfloat16), "fsdp", scatter_dimension=0, tiled=True
        ).astype(jnp.float32),
        lax.psum_scatter(
            grad_ffn.astype(jnp.bfloat16), "fsdp", scatter_dimension=0, tiled=True
        ).astype(jnp.float32),
    )
    resid_b = grad_resid.astype(jnp.bfloat16)
    grad_attn_w = jnp.dot(attn_b.T, resid_b, preferred_element_type=jnp.float32)
    grad_mixed = (
        jnp.dot(resid_b, back_attn.T, preferred_element_type=jnp.float32)
        .astype(jnp.bfloat16)
        .reshape(seq_dev, tok_seq, HEADS, HEAD_DIM)
    )
    row_delta = jnp.sum(grad_mixed.astype(jnp.float32) * attn_f, axis=-1)
    zero_q = jnp.zeros((seq_dev, tok_seq, HEADS, HEAD_DIM), jnp.float32)
    zero_kv = jnp.zeros((seq_dev, seq_len, HEADS, HEAD_DIM), jnp.float32)

    def backward_step(state_in, block_index):
        grad_q_sum, grad_key_all, grad_value_all = state_in
        begin = block_index * block_len
        key_piece = lax.dynamic_slice_in_dim(whole_keys, begin, block_len, 1)
        value_piece = lax.dynamic_slice_in_dim(whole_values, begin, block_len, 1)
        grad_query, grad_keys, grad_values = back_piece(
            queries, grad_mixed, log_sum, row_delta, key_piece, value_piece, scale_factor
        )
        return (
            (
                grad_q_sum + grad_query,
                add_at(grad_key_all, grad_keys, begin),
                add_at(grad_value_all, grad_values, begin),
            ),
            None,
        )

    back_state, unused_back = lax.scan(
        backward_step, (zero_q, zero_kv, zero_kv), jnp.arange(blocks_num, dtype=jnp.int32)
    )
    grad_q_sum, grad_key_all, grad_value_all = back_state
    own_keys, own_values = (
        lax.psum_scatter(
            grad_key_all.astype(jnp.bfloat16), "ctx", scatter_dimension=1, tiled=True
        ).astype(jnp.float32),
        lax.psum_scatter(
            grad_value_all.astype(jnp.bfloat16), "ctx", scatter_dimension=1, tiled=True
        ).astype(jnp.float32),
    )
    grad_q_rot = rotate_back(grad_q_sum, cosine, sine_part).reshape(row_count, D)
    grad_k_rot = rotate_back(own_keys, cosine, sine_part).reshape(row_count, D)
    grad_joint = jnp.concatenate(
        [grad_q_rot, grad_k_rot, own_values.reshape(row_count, D)], axis=-1
    ).astype(jnp.bfloat16)
    grad_qkv = jnp.dot(input_one.T, grad_joint, preferred_element_type=jnp.float32)
    grad_normed_one = jnp.dot(grad_joint, back_qkv.T, preferred_element_type=jnp.float32)
    grad_g1 = jnp.sum(grad_normed_one * normed_one, axis=0)
    grad_input = grad_resid + norm_back(
        grad_normed_one * back_g1.astype(jnp.float32), normed_one, inv_one
    )
    part_g1, part_qkv, part_attn = (
        lax.psum_scatter(
            grad_g1.astype(jnp.bfloat16), "fsdp", scatter_dimension=0, tiled=True
        ).astype(jnp.float32),
        lax.psum_scatter(
            grad_qkv.astype(jnp.bfloat16), "fsdp", scatter_dimension=0, tiled=True
        ).astype(jnp.float32),
        lax.psum_scatter(
            grad_attn_w.astype(jnp.bfloat16), "fsdp", scatter_dimension=0, tiled=True
        ).astype(jnp.float32),
    )
    totals = (
        lax.psum(part_g1.astype(jnp.bfloat16), "ctx").astype(jnp.float32),
        lax.psum(part_qkv.astype(jnp.bfloat16), "ctx").astype(jnp.float32),
        lax.psum(part_attn.astype(jnp.bfloat16), "ctx").astype(jnp.float32),
        lax.psum(part_g2.astype(jnp.bfloat16), "ctx").astype(jnp.float32),
        lax.psum(part_in.astype(jnp.bfloat16), "ctx").astype(jnp.float32),
        lax.psum(part_ffn.astype(jnp.bfloat16), "ctx").astype(jnp.float32),
    )
    return (
        output.reshape(seq_dev, tok_seq, D),
        grad_input.reshape(seq_dev, tok_seq, D),
        totals[0],
        totals[1],
        totals[2],
        totals[3],
        totals[4],
        totals[5],
    )


def solution(mesh):
    return jax.shard_map(
        on_device,
        mesh=mesh,
        in_specs=(
            P("fsdp", "ctx", None),
            P("fsdp"),
            P("fsdp", None),
            P("fsdp", None),
            P("fsdp"),
            P("fsdp", None),
            P("fsdp", None),
            P("fsdp", "ctx", None),
        ),
        out_specs=(
            P("fsdp", "ctx", None),
            P("fsdp", "ctx", None),
            P("fsdp"),
            P("fsdp", None),
            P("fsdp", None),
            P("fsdp"),
            P("fsdp", None),
            P("fsdp", None),
        ),
        check_vma=False,
    )
```

profile of v0, /device:TPU:0, one launch (start us, length us, event | category | flops | bytes accessed | tf_op | source)
XLA Modules:
  0.0 1007.0 jit_solution(11697671415666420469)
XLA Ops:
  8.6 6.0 all-gather.1
  16.9 41.8 %all-gather.10.cloned.1.call-done = bf16[1024,3072]{1,0:T(8,128)(2,1)} async-done(((bf16[256,3072]{1,0:T(8,128)(2,1)}), bf16[1024,3072]{1,0:T(8,128)(2,1)}) %all-gather.10.cloned.1.call-update) | async-done | bytes 6291472 | tf_op jit(solution)/shard_map/all_gather | solution.py:122
  58.7 8.7 copy.36
  67.4 4.7 fusion.61
  83.7 5.6 all-gather.2
  89.3 59.0 %all-gather.20.cloned.1.call-done = bf16[2,512,1,16,64]{4,3,2,0,1:T(8,128)(2,1)} async-done(((bf16[2,64,1,16,64]{4,3,2,0,1:T(8,128)(2,1)}), bf16[2,512,1,16,64]{4,3,2,0,1:T(8,128)(2,1)}) %all-gather.20.cloned.1.call-update) | async-done | bytes 2097168 | tf_op jit(solution)/shard_map/all_gather | solution.py:145
  148.3 5.4 copy.42
  153.7 68.6 %all-gather.12.cloned.1.call-done = bf16[2,512,16,64]{3,2,0,1:T(8,128)(2,1)} async-done(((bf16[2,64,16,64]{3,2,0,1:T(8,128)(2,1)}), bf16[2,512,16,64]{3,2,0,1:T(8,128)(2,1)}) %all-gather.12.cloned.1.call-update) | async-done | bytes 2097168 | tf_op jit(solution)/shard_map/all_gather | solution.py:144
  222.4 4.5 copy.48
  233.8 11.1 %all-gather.14.cloned.1.call-done = bf16[1024,1024]{1,0:T(8,128)(2,1)} async-done(((bf16[256,1024]{1,0:T(8,128)(2,1)}), bf16[1024,1024]{1,0:T(8,128)(2,1)}) %all-gather.14.cloned.1.call-update) | async-done | bytes 2097168 | tf_op jit(solution)/shard_map/all_gather | solution.py:123
  247.3 70.8 %all-gather.16.cloned.1.call-done = bf16[1024,5248]{1,0:T(8,128)(2,1)} async-done(((bf16[256,5248]{1,0:T(8,128)(2,1)}), bf16[1024,5248]{1,0:T(8,128)(2,1)}) %all-gather.16.cloned.1.call-update) | async-done | bytes 10747920 | tf_op jit(solution)/shard_map/all_gather | solution.py:125
  318.0 7.3 fusion.73
  325.3 35.3 %all-gather.18.cloned.1.call-done = bf16[2624,1024]{1,0:T(8,128)(2,1)} async-done(((bf16[656,1024]{1,0:T(8,128)(2,1)}), bf16[2624,1024]{1,0:T(8,128)(2,1)}) %all-gather.18.cloned.1.call-update) | async-done | bytes 5373968 | tf_op jit(solution)/shard_map/all_gather | solution.py:126
  360.6 8.5 multiply_convert_fusion.1
  378.8 4.2 fusion.1
  386.4 7.4 copy.56
  393.9 6.8 reshape.175
  400.7 4.4 convert_bitcast_fusion
  405.1 7.4 copy.58
  412.5 6.8 reshape.177
  433.2 35.9 %reduce-scatter.19.cloned.1.call-done = bf16[64,2048]{1,0:T(8,128)(2,1)} async-done(((bf16[512,2048]{1,0:T(8,128)(2,1)}), bf16[64,2048]{1,0:T(8,128)(2,1)}) %reduce-scatter.19.cloned.1.call-update) | async-done | bytes 262160
  473.1 67.0 %reduce-scatter.21.cloned.1.call-done = bf16[64,2048]{1,0:T(8,128)(2,1)} async-done(((bf16[512,2048]{1,0:T(8,128)(2,1)}), bf16[64,2048]{1,0:T(8,128)(2,1)}) %reduce-scatter.21.cloned.1.call-update) | async-done | bytes 262160
  542.9 5.1 multiply_reduce_fusion.2
  548.0 4.4 convolution_convert_fusion.2
  553.6 7.0 convolution_convert_fusion
  560.6 12.2 %reduce-scatter.13.cloned.1.call-done = bf16[256,1024]{1,0:T(8,128)(2,1)} async-done(((bf16[1024,1024]{1,0:T(8,128)(2,1)}), bf16[256,1024]{1,0:T(8,128)(2,1)}) %reduce-scatter.13.cloned.1.call-update) | async-done | bytes 524304 | tf_op jit(solution)/shard_map/reduce_scatter | solution.py:251
  572.8 55.2 %reduce-scatter.17.cloned.1.call-done = bf16[656,1024]{1,0:T(8,128)(2,1)} async-done(((bf16[2624,1024]{1,0:T(8,128)(2,1)}), bf16[656,1024]{1,0:T(8,128)(2,1)}) %reduce-scatter.17.cloned.1.call-update) | async-done | bytes 1343504 | tf_op jit(solution)/shard_map/reduce_scatter | solution.py:189
  628.0 61.4 %reduce-scatter.11.cloned.1.call-done = bf16[256,3072]{1,0:T(8,128)(2,1)} async-done(((bf16[1024,3072]{1,0:T(8,128)(2,1)}), bf16[256,3072]{1,0:T(8,128)(2,1)}) %reduce-scatter.11.cloned.1.call-update) | async-done | bytes 1572880 | tf_op jit(solution)/shard_map/reduce_scatter | solution.py:248
  689.4 88.5 %reduce-scatter.15.cloned.1.call-done = bf16[256,5248]{1,0:T(8,128)(2,1)} async-done(((bf16[1024,5248]{1,0:T(8,128)(2,1)}), bf16[256,5248]{1,0:T(8,128)(2,1)}) %reduce-scatter.15.cloned.1.call-update) | async-done | bytes 2686992 | tf_op jit(solution)/shard_map/reduce_scatter | solution.py:186
  784.0 5.7 all-reduce.4
  789.9 22.8 %all-reduce.2 = (bf16[256]{0:T(256)(128)(2,1)S(1)}, bf16[256]{0:T(256)(128)(2,1)S(1)}) all-reduce(bf16[256]{0:T(256)(128)(2,1)S(1)} %dynamic-slice.1, bf16[256]{0:T(256)(128)(2,1)S(1)} %dynamic-slice.3), channel_id=1, replica_groups=mesh['ctx'=8,'fsdp'=4] {'ctx'}, use_global_device_ids=true, to_apply=%region_15.16 | all-reduce | flops 512 | bytes 2048 | tf_op jit(solution)/shard_map/psum | solution.py:256
  814.9 175.5 %all-reduce.7.cloned.1.call-done = (bf16[256,3072]{1,0:T(8,128)(2,1)}, bf16[256,1024]{1,0:T(8,128)(2,1)}, bf16[256,5248]{1,0:T(8,128)(2,1)}, bf16[656,1024]{1,0:T(8,128)(2,1)}) async-done(((bf16[256,3072]{1,0:T(8,128)(2,1)}, bf16[256,1024]{1,0:T(8,128)(2,1)}, bf16[256,5248]{1,0:T(8,128)(2,1)}, bf16[656,1024]{1,0:T(8,128)(2,1)}), (bf16[256,3072]{1,0:T(8,128)(2,1)}, bf16[256,1024]{1,0:T(8,128)(2,1)}, ...) | async-done | bytes 6127632 | tf_op jit(solution)/shard_map/psum | solution.py:257
  (150 shorter events, 76.7 us)
Async XLA Ops:
  7.2 51.5 %all-gather.10.cloned.1.call-start = ((), (), s32[]{:S(2)}) async-start(), calls=%async_computation.6 | async-start | bytes 7864320 | tf_op jit(solution)/shard_map/all_gather | solution.py:122
  7.9 140.4 %all-gather.20.cloned.1.call-start = ((), (), s32[]{:S(2)}) async-start(), calls=%async_computation.15 | async-start | bytes 4718592 | tf_op jit(solution)/shard_map/all_gather | solution.py:145
  58.7 8.7 copy-start.10
  72.1 1.7 copy-start.8
  75.4 146.9 %all-gather.12.cloned.1.call-start = ((), (), s32[]{:S(2)}) async-start(), calls=%async_computation.7 | async-start | bytes 4718592 | tf_op jit(solution)/shard_map/all_gather | solution.py:144
  78.0 1.9 copy-start.9
  80.4 146.5 %copy-start.12 = (bf16[2,64,16,64]{1,3,2,0:T(8,128)(2,1)}, bf16[2,64,16,64]{1,3,2,0:T(8,128)(2,1)S(1)}, u32[]{:S(2)}) copy-start(bf16[2,64,16,64]{1,3,2,0:T(8,128)(2,1)S(1)} %get-tuple-element.76) | copy-start | bytes 786436
  81.9 163.0 %all-gather.14.cloned.1.call-start = ((), (), s32[]{:S(2)}) async-start(), calls=%async_computation.8 | async-start | bytes 2621440 | tf_op jit(solution)/shard_map/all_gather | solution.py:123
  82.5 235.5 %all-gather.16.cloned.1.call-start = ((), (), s32[]{:S(2)}) async-start(), calls=%async_computation.9 | async-start | bytes 13434880 | tf_op jit(solution)/shard_map/all_gather | solution.py:125
  83.1 277.5 %all-gather.18.cloned.1.call-start = ((), (), s32[]{:S(2)}) async-start(), calls=%async_computation.10 | async-start | bytes 6717440 | tf_op jit(solution)/shard_map/all_gather | solution.py:126
  83.7 385.4 %reduce-scatter.19.cloned.1.call-start = ((), (), s32[]{:S(2)}) async-start(), calls=%async_computation.16 | async-start | bytes 2359296
  227.7 2.2 copy-start
  227.7 3.2 copy-start.3
  318.0 42.6 %copy-start.17 = (bf16[2,64,1024]{2,1,0:T(8,128)(2,1)S(1)}, bf16[2,64,1024]{2,1,0:T(8,128)(2,1)}, u32[]{:S(2)}) copy-start(bf16[2,64,1024]{2,1,0:T(8,128)(2,1)} %param.15) | copy-start | bytes 786436
  360.6 8.5 copy-start.2
  369.1 3.7 copy-start.19
  369.1 3.7 copy-start.21
  369.1 4.8 copy-start.4
  378.8 5.6 copy-start.13
  383.1 1.3 copy-start.1
  400.6 139.4 %reduce-scatter.21.cloned.1.call-start = ((), (), s32[]{:S(2)}) async-start(), calls=%async_computation.17 | async-start | bytes 2359296
  419.3 153.5 %reduce-scatter.13.cloned.1.call-start = ((), (), s32[]{:S(2)}) async-start(), calls=%async_computation.12 | async-start | bytes 2621440 | tf_op jit(solution)/shard_map/reduce_scatter | solution.py:251
  422.5 205.5 %reduce-scatter.17.cloned.1.call-start = ((), (), s32[]{:S(2)}) async-start(), calls=%async_computation.14 | async-start | bytes 6717440 | tf_op jit(solution)/shard_map/reduce_scatter | solution.py:189
  422.5 2.3 copy-start.18
  428.8 260.6 %reduce-scatter.11.cloned.1.call-start = ((), (), s32[]{:S(2)}) async-start(), calls=%async_computation.11 | async-start | bytes 7864320 | tf_op jit(solution)/shard_map/reduce_scatter | solution.py:248
  472.0 70.9 %copy-start.11 = (bf16[2,64,1024]{2,1,0:T(8,128)(2,1)S(1)}, bf16[2,64,1024]{2,1,0:T(8,128)(2,1)}, u32[]{:S(2)}) copy-start(bf16[2,64,1024]{2,1,0:T(8,128)(2,1)} %param.8) | copy-start | bytes 786436
  552.5 225.5 %reduce-scatter.15.cloned.1.call-start = ((), (), s32[]{:S(2)}) async-start(), calls=%async_computation.13 | async-start | bytes 13434880 | tf_op jit(solution)/shard_map/reduce_scatter | solution.py:186
  560.6 429.8 %all-reduce.7.cloned.1.call-start = ((), (), s32[]{:S(2)}) async-start(), calls=%async_computation.18 | async-start | bytes 12255232 | tf_op jit(solution)/shard_map/psum | solution.py:257
  779.8 34.0 %copy-start.7 = (f32[128,1024]{1,0:T(8,128)S(1)}, f32[128,1024]{1,0:T(8,128)}, u32[]{:S(2)}) copy-start(f32[128,1024]{1,0:T(8,128)} %copy-done.5) | copy-start | bytes 1572868
  990.4 2.2 copy-start.15
  992.7 2.0 copy-start.16
  994.7 2.7 copy-start.14
  (6 other events, 5.6 us)
Sparse Core Ops, SparseCore 0:
  9.5 49.1 all-gather.9
  75.5 72.7 all-gather.19
  151.0 71.3 all-gather.11
  223.8 21.0 all-gather.13
  246.3 71.6 all-gather.15
  319.4 41.1 all-gather.17
  400.8 68.2 reduce-scatter.18
  472.6 67.3 reduce-scatter.20
  542.6 30.1 reduce-scatter.12
  575.8 52.1 reduce-scatter.16
  630.5 58.8 reduce-scatter.10
  691.9 85.9 reduce-scatter.14
  782.6 207.7 all-reduce.6
where the time goes:
time: 1010 us
  waiting for transfers between devices  785 us (78%)
  local copies, waits for them, and re-layouts  75.1 us (7%)
  matrix products  69.9 us (7%)
  blocking collectives  40.1 us (4%)
  other arithmetic  20.9 us (2%)
  between operations  15.3 us (2%)
    psum x1, waiting for transfers between devices, on_device(): lax.psum(part_qkv.astype(jnp.bfloat16), 'ctx').astype(jnp.float32)  176 us
    unnamed x15, waiting for transfers between devices  105 us
    reduce_scatter x1, waiting for transfers between devices, on_device(): lax.psum_scatter(grad_in.astype(jnp.bfloat16), 'fsdp', scatter_dimension=...  88.5 us
    all_gather x1, waiting for transfers between devices, on_device(): lax.all_gather(w_in, 'fsdp', axis=0, tiled=True)  70.8 us
    all_gather x1, waiting for transfers between devices, on_device(): lax.all_gather(key_rows, 'ctx', axis=1, tiled=True)  68.6 us
    reduce_scatter x1, waiting for transfers between devices, on_device(): lax.psum_scatter(grad_qkv.astype(jnp.bfloat16), 'fsdp', scatter_dimension...  61.4 us
    all_gather x1, waiting for transfers between devices, on_device(): lax.all_gather(value_rows, 'ctx', axis=1, tiled=True)  59 us
    reduce_scatter x1, waiting for transfers between devices, on_device(): lax.psum_scatter(grad_ffn.astype(jnp.bfloat16), 'fsdp', scatter_dimension...  55.2 us
  transfers between devices with their start and end apart: 13, of which 13 were waited for; matrix products, arithmetic and copies ran while one was open for 9% of the time, Pallas kernels for 0%

commit v1 on v0

--- a/solution.py
+++ b/solution.py
@@ -10,6 +10,18 @@
 FF = 2624
 EPSILON = 1e-05
 ROPE_THETA = 160000.0
+
+
+def gather_by_bits(value, axis, dim):
+    ways, here = (lax.axis_size(axis), lax.axis_index(axis))
+    grown, reach = (value, 1)
+    while reach < ways:
+        theirs = lax.ppermute(grown, axis, [(d, d ^ reach) for d in range(ways)])
+        mine_first = jnp.concatenate([grown, theirs], axis=dim)
+        theirs_first = jnp.concatenate([theirs, grown], axis=dim)
+        grown = jnp.where(here & reach == 0, mine_first, theirs_first)
+        reach = 2 * reach
+    return grown
 
 
 def norm_parts(values_in):
@@ -142,7 +154,7 @@
     )
     whole_keys, whole_values = (
         lax.all_gather(key_rows, "ctx", axis=1, tiled=True),
-        lax.all_gather(value_rows, "ctx", axis=1, tiled=True),
+        gather_by_bits(value_rows, "ctx", 1),
     )
 
     def forward_step(state_in, block_index):

time: 1010 us -> 989 us (0.979)
  waiting for transfers between devices: 785 us -> 760 us
  local copies, waits for them, and re-layouts: 75.1 us -> 64 us
    all_gather x1 -> x0, waiting for transfers between devices: 59 us -> none  [on_device(): lax.all_gather(value_rows, 'ctx', axis=1, tiled=True)]
    ppermute x0 -> x3, waiting for transfers between devices: none -> 36.2 us  [gather_by_bits(): theirs = lax.ppermute(grown, axis, [(d, d ^ reach) for d in range(ways)])]
    unnamed x64 -> x68, local copies, waits for them, and re-layouts: 45.5 us -> 39.9 us
    unnamed x15 -> x14, waiting for transfers between devices: 105 us -> 106 us
  transfers between devices with their start and end apart: 13 -> 15, of which waited for: 13 -> 14; matrix products, arithmetic and copies ran while one was open for 9% -> 9% of each run, Pallas kernels for 0% -> 0%
where the time goes in v1:
time: 989 us; the launch traced here: 984 us
  waiting for transfers between devices  760 us (77%)
  matrix products  75.2 us (8%)
  local copies, waits for them, and re-layouts  64 us (6%)
  blocking collectives  40.1 us (4%)
  other arithmetic  22.3 us (2%)
  between operations  15.6 us (2%)
    psum x1, waiting for transfers between devices, on_device(): lax.psum(part_qkv.astype(jnp.bfloat16), 'ctx').astype(jnp.float32)  175 us
    unnamed x14, waiting for transfers between devices  106 us
    reduce_scatter x1, waiting for transfers between devices, on_device(): lax.psum_scatter(grad_in.astype(jnp.bfloat16), 'fsdp', scatter_dimension=...  88.6 us
    all_gather x1, waiting for transfers between devices, on_device(): lax.all_gather(w_in, 'fsdp', axis=0, tiled=True)  70.8 us
    all_gather x1, waiting for transfers between devices, on_device(): lax.all_gather(key_rows, 'ctx', axis=1, tiled=True)  66.2 us
    reduce_scatter x1, waiting for transfers between devices, on_device(): lax.psum_scatter(grad_qkv.astype(jnp.bfloat16), 'fsdp', scatter_dimension...  61.3 us
    reduce_scatter x1, waiting for transfers between devices, on_device(): lax.psum_scatter(grad_ffn.astype(jnp.bfloat16), 'fsdp', scatter_dimension...  55.4 us
    all_gather x1, waiting for transfers between devices, on_device(): lax.all_gather(w_qkv, 'fsdp', axis=0, tiled=True)  42.5 us
  transfers between devices with their start and end apart: 15, of which 14 were waited for; matrix products, arithmetic and copies ran while one was open for 9% of the time, Pallas kernels for 0%

profile of v1, /device:TPU:0, one launch (start us, length us, event | category | flops | bytes accessed | tf_op | source)
XLA Modules:
  0.0 983.8 jit_solution(11337642966304465326)
XLA Ops:
  8.6 6.0 all-gather
  16.2 42.5 %all-gather.8.cloned.1.call-done = bf16[1024,3072]{1,0:T(8,128)(2,1)} async-done(((bf16[256,3072]{1,0:T(8,128)(2,1)}), bf16[1024,3072]{1,0:T(8,128)(2,1)}) %all-gather.8.cloned.1.call-update) | async-done | bytes 6291472 | tf_op jit(solution)/shard_map/all_gather | solution.py:134
  58.7 8.6 copy.36
  67.3 4.7 fusion.54
  80.6 18.2 %collective-permute-done = bf16[2,64,16,64]{1,3,2,0:T(8,128)(2,1)S(1)} collective-permute-done((bf16[2,64,16,64]{1,3,2,0:T(8,128)(2,1)S(1)}, bf16[2,64,16,64]{1,3,2,0:T(8,128)(2,1)S(1)}, u32[]{:S(2)}, u32[]{:S(2)}) %collective-permute-start) | collective-permute-done | bytes 262176 | tf_op jit(solution)/shard_map/ppermute | solution.py:19
  100.9 17.9 %collective-permute-done.1 = bf16[2,128,16,64]{1,3,2,0:T(8,128)(2,1)S(1)} collective-permute-done((bf16[2,128,16,64]{1,3,2,0:T(8,128)(2,1)S(1)}, bf16[2,128,16,64]{1,3,2,0:T(8,128)(2,1)S(1)}, u32[]{:S(2)}, u32[]{:S(2)}) %collective-permute-start.1) | collective-permute-done | bytes 524320 | tf_op jit(solution)/shard_map/ppermute | solution.py:19
  122.7 5.6 all-gather.1
  128.3 66.2 %all-gather.10.cloned.1.call-done = bf16[2,512,16,64]{3,2,0,1:T(8,128)(2,1)} async-done(((bf16[2,64,16,64]{3,2,0,1:T(8,128)(2,1)}), bf16[2,512,16,64]{3,2,0,1:T(8,128)(2,1)}) %all-gather.10.cloned.1.call-update) | async-done | bytes 2097168 | tf_op jit(solution)/shard_map/all_gather | solution.py:156
  194.6 4.5 copy.46
  201.9 4.9 fusion.72
  207.6 10.0 %all-gather.12.cloned.1.call-done = bf16[1024,1024]{1,0:T(8,128)(2,1)} async-done(((bf16[256,1024]{1,0:T(8,128)(2,1)}), bf16[1024,1024]{1,0:T(8,128)(2,1)}) %all-gather.12.cloned.1.call-update) | async-done | bytes 2097168 | tf_op jit(solution)/shard_map/all_gather | solution.py:135
  219.9 70.8 %all-gather.14.cloned.1.call-done = bf16[1024,5248]{1,0:T(8,128)(2,1)} async-done(((bf16[256,5248]{1,0:T(8,128)(2,1)}), bf16[1024,5248]{1,0:T(8,128)(2,1)}) %all-gather.14.cloned.1.call-update) | async-done | bytes 10747920 | tf_op jit(solution)/shard_map/all_gather | solution.py:137
  290.7 7.3 fusion.68
  297.9 35.3 %all-gather.16.cloned.1.call-done = bf16[2624,1024]{1,0:T(8,128)(2,1)} async-done(((bf16[656,1024]{1,0:T(8,128)(2,1)}), bf16[2624,1024]{1,0:T(8,128)(2,1)}) %all-gather.16.cloned.1.call-update) | async-done | bytes 5373968 | tf_op jit(solution)/shard_map/all_gather | solution.py:138
  333.3 8.5 multiply_convert_fusion.1
  353.8 5.4 fusion.1
  362.6 7.4 copy.54
  370.0 6.8 reshape.174
  376.9 4.5 convert_bitcast_fusion
  381.4 7.4 copy.56
  388.8 6.8 reshape.176
  408.7 36.6 %reduce-scatter.19.cloned.1.call-done = bf16[64,2048]{1,0:T(8,128)(2,1)} async-done(((bf16[512,2048]{1,0:T(8,128)(2,1)}), bf16[64,2048]{1,0:T(8,128)(2,1)}) %reduce-scatter.19.cloned.1.call-update) | async-done | bytes 262160
  449.3 67.2 %reduce-scatter.21.cloned.1.call-done = bf16[64,2048]{1,0:T(8,128)(2,1)} async-done(((bf16[512,2048]{1,0:T(8,128)(2,1)}), bf16[64,2048]{1,0:T(8,128)(2,1)}) %reduce-scatter.21.cloned.1.call-update) | async-done | bytes 262160
  519.4 5.1 multiply_reduce_fusion.2
  530.0 7.0 convolution_convert_fusion
  537.1 12.2 %reduce-scatter.13.cloned.1.call-done = bf16[256,1024]{1,0:T(8,128)(2,1)} async-done(((bf16[1024,1024]{1,0:T(8,128)(2,1)}), bf16[256,1024]{1,0:T(8,128)(2,1)}) %reduce-scatter.13.cloned.1.call-update) | async-done | bytes 524304 | tf_op jit(solution)/shard_map/reduce_scatter | solution.py:263
  549.3 55.4 %reduce-scatter.17.cloned.1.call-done = bf16[656,1024]{1,0:T(8,128)(2,1)} async-done(((bf16[2624,1024]{1,0:T(8,128)(2,1)}), bf16[656,1024]{1,0:T(8,128)(2,1)}) %reduce-scatter.17.cloned.1.call-update) | async-done | bytes 1343504 | tf_op jit(solution)/shard_map/reduce_scatter | solution.py:201
  604.7 61.3 %reduce-scatter.11.cloned.1.call-done = bf16[256,3072]{1,0:T(8,128)(2,1)} async-done(((bf16[1024,3072]{1,0:T(8,128)(2,1)}), bf16[256,3072]{1,0:T(8,128)(2,1)}) %reduce-scatter.11.cloned.1.call-update) | async-done | bytes 1572880 | tf_op jit(solution)/shard_map/reduce_scatter | solution.py:260
  665.9 88.6 %reduce-scatter.15.cloned.1.call-done = bf16[256,5248]{1,0:T(8,128)(2,1)} async-done(((bf16[1024,5248]{1,0:T(8,128)(2,1)}), bf16[256,5248]{1,0:T(8,128)(2,1)}) %reduce-scatter.15.cloned.1.call-update) | async-done | bytes 2686992 | tf_op jit(solution)/shard_map/reduce_scatter | solution.py:198
  760.7 5.7 all-reduce.4
  766.6 22.7 %all-reduce.2 = (bf16[256]{0:T(256)(128)(2,1)S(1)}, bf16[256]{0:T(256)(128)(2,1)S(1)}) all-reduce(bf16[256]{0:T(256)(128)(2,1)S(1)} %dynamic-slice.1, bf16[256]{0:T(256)(128)(2,1)S(1)} %dynamic-slice.3), channel_id=1, replica_groups=mesh['ctx'=8,'fsdp'=4] {'ctx'}, use_global_device_ids=true, to_apply=%region_15.16 | all-reduce | flops 512 | bytes 2048 | tf_op jit(solution)/shard_map/psum | solution.py:268
  791.5 175.4 %all-reduce.7.cloned.1.call-done = (bf16[256,3072]{1,0:T(8,128)(2,1)}, bf16[256,1024]{1,0:T(8,128)(2,1)}, bf16[256,5248]{1,0:T(8,128)(2,1)}, bf16[656,1024]{1,0:T(8,128)(2,1)}) async-done(((bf16[256,3072]{1,0:T(8,128)(2,1)}, bf16[256,1024]{1,0:T(8,128)(2,1)}, bf16[256,5248]{1,0:T(8,128)(2,1)}, bf16[656,1024]{1,0:T(8,128)(2,1)}), (bf16[256,3072]{1,0:T(8,128)(2,1)}, bf16[256,1024]{1,0:T(8,128)(2,1)}, ...) | async-done | bytes 6127632 | tf_op jit(solution)/shard_map/psum | solution.py:269
  (157 shorter events, 81.6 us)
Async XLA Ops:
  7.2 8.8 copy-start.7
  7.2 51.5 %all-gather.8.cloned.1.call-start = ((), (), s32[]{:S(2)}) async-start(), calls=%async_computation.6 | async-start | bytes 7864320 | tf_op jit(solution)/shard_map/all_gather | solution.py:134
  7.9 186.7 %all-gather.10.cloned.1.call-start = ((), (), s32[]{:S(2)}) async-start(), calls=%async_computation.7 | async-start | bytes 4718592 | tf_op jit(solution)/shard_map/all_gather | solution.py:156
  15.9 51.4 %copy-start.20 = (f32[2,64]{1,0:T(2,128)}, f32[2,64]{1,0:T(2,128)S(1)}, u32[]{:S(2)}) copy-start(f32[2,64]{1,0:T(2,128)S(1)} %broadcast_multiply_fusion.3) | copy-start | bytes 1540
  16.2 51.1 %copy-start.23 = (f32[2,64]{1,0:T(2,128)}, f32[2,64]{1,0:T(2,128)S(1)}, u32[]{:S(2)}) copy-start(f32[2,64]{1,0:T(2,128)S(1)} %add_rsqrt_fusion) | copy-start | bytes 1540
  74.2 124.8 %copy-start.9 = (bf16[2,64,16,64]{1,3,2,0:T(8,128)(2,1)}, bf16[2,64,16,64]{1,3,2,0:T(8,128)(2,1)S(1)}, u32[]{:S(2)}) copy-start(bf16[2,64,16,64]{1,3,2,0:T(8,128)(2,1)S(1)} %get-tuple-element.76) | copy-start | bytes 786436
  75.8 141.8 %all-gather.12.cloned.1.call-start = ((), (), s32[]{:S(2)}) async-start(), calls=%async_computation.8 | async-start | bytes 2621440 | tf_op jit(solution)/shard_map/all_gather | solution.py:135
  76.5 214.2 %all-gather.14.cloned.1.call-start = ((), (), s32[]{:S(2)}) async-start(), calls=%async_computation.9 | async-start | bytes 13434880 | tf_op jit(solution)/shard_map/all_gather | solution.py:137
  77.1 256.2 %all-gather.16.cloned.1.call-start = ((), (), s32[]{:S(2)}) async-start(), calls=%async_computation.10 | async-start | bytes 6717440 | tf_op jit(solution)/shard_map/all_gather | solution.py:138
  77.7 367.6 %reduce-scatter.19.cloned.1.call-start = ((), (), s32[]{:S(2)}) async-start(), calls=%async_computation.15 | async-start | bytes 2359296
  79.0 43.7 %copy-start.25 = (bf16[256]{0:T(256)(128)(2,1)S(1)}, bf16[256]{0:T(256)(128)(2,1)}, u32[]{:S(2)}) copy-start(bf16[256]{0:T(256)(128)(2,1)} %param.12) | copy-start | bytes 1540
  79.0 19.8 %collective-permute-start = (bf16[2,64,16,64]{1,3,2,0:T(8,128)(2,1)S(1)}, bf16[2,64,16,64]{1,3,2,0:T(8,128)(2,1)S(1)}, u32[]{:S(2)}, u32[]{:S(2)}) collective-permute-start(bf16[2,64,16,64]{1,3,2,0:T(8,128)(2,1)S(1)} %fusion.51), channel_id=1, source_target_pairs={{0,4},{4,0},{8,12},{12,8},{16,20},{20,16},{24,28},{28,24},{1,5},{5... | collective-permute-start | bytes 786440 | tf_op jit(solution)/shard_map/ppermute | solution.py:19
  99.4 19.5 %collective-permute-start.1 = (bf16[2,128,16,64]{1,3,2,0:T(8,128)(2,1)S(1)}, bf16[2,128,16,64]{1,3,2,0:T(8,128)(2,1)S(1)}, u32[]{:S(2)}, u32[]{:S(2)}) collective-permute-start(bf16[2,128,16,64]{1,3,2,0:T(8,128)(2,1)S(1)} %maximum_select_fusion.2), channel_id=1, source_target_pairs={{0,8},{4,12},{8,0},{12,4},{16,24},{20,28},{24,16},{28,20},{1,9},{5... | collective-permute-start | bytes 1572872 | tf_op jit(solution)/shard_map/ppermute | solution.py:19
  120.3 81.5 %collective-permute-start.2 = (bf16[2,256,16,64]{1,3,2,0:T(8,128)(2,1)}, bf16[2,256,16,64]{1,3,2,0:T(8,128)(2,1)}, u32[]{:S(2)}, u32[]{:S(2)}) collective-permute-start(bf16[2,256,16,64]{1,3,2,0:T(8,128)(2,1)} %maximum_select_fusion.1), channel_id=1, source_target_pairs={{0,16},{4,20},{8,24},{12,28},{16,0},{20,4},{24,8},{28,12},{1,17},{... | collective-permute-start | bytes 3145736 | tf_op jit(solution)/shard_map/ppermute | solution.py:19
  290.7 42.6 %copy-start.14 = (bf16[2,64,1024]{2,1,0:T(8,128)(2,1)S(1)}, bf16[2,64,1024]{2,1,0:T(8,128)(2,1)}, u32[]{:S(2)}) copy-start(bf16[2,64,1024]{2,1,0:T(8,128)(2,1)} %param.15) | copy-start | bytes 786436
  333.3 8.5 copy-start.1
  341.7 4.3 copy-start.17
  341.7 4.3 copy-start.19
  341.8 4.2 copy-start.15
  341.8 4.5 copy-start.3
  346.3 49.6 %copy-start.4 = (f32[128,1024]{1,0:T(8,128)}, f32[128,1024]{1,0:T(8,128)S(1)}, u32[]{:S(2)}) copy-start(f32[128,1024]{1,0:T(8,128)S(1)} %multiply_add_fusion.1) | copy-start | bytes 1572868
  353.8 6.8 copy-start.10
  376.8 139.7 %reduce-scatter.21.cloned.1.call-start = ((), (), s32[]{:S(2)}) async-start(), calls=%async_computation.16 | async-start | bytes 2359296
  395.6 153.7 %reduce-scatter.13.cloned.1.call-start = ((), (), s32[]{:S(2)}) async-start(), calls=%async_computation.12 | async-start | bytes 2621440 | tf_op jit(solution)/shard_map/reduce_scatter | solution.py:263
  398.0 206.7 %reduce-scatter.17.cloned.1.call-start = ((), (), s32[]{:S(2)}) async-start(), calls=%async_computation.14 | async-start | bytes 6717440 | tf_op jit(solution)/shard_map/reduce_scatter | solution.py:201
  404.4 261.5 %reduce-scatter.11.cloned.1.call-start = ((), (), s32[]{:S(2)}) async-start(), calls=%async_computation.11 | async-start | bytes 7864320 | tf_op jit(solution)/shard_map/reduce_scatter | solution.py:260
  448.2 71.2 %copy-start.8 = (bf16[2,64,1024]{2,1,0:T(8,128)(2,1)S(1)}, bf16[2,64,1024]{2,1,0:T(8,128)(2,1)}, u32[]{:S(2)}) copy-start(bf16[2,64,1024]{2,1,0:T(8,128)(2,1)} %param.8) | copy-start | bytes 786436
  529.0 225.6 %reduce-scatter.15.cloned.1.call-start = ((), (), s32[]{:S(2)}) async-start(), calls=%async_computation.13 | async-start | bytes 13434880 | tf_op jit(solution)/shard_map/reduce_scatter | solution.py:198
  537.1 429.9 %all-reduce.7.cloned.1.call-start = ((), (), s32[]{:S(2)}) async-start(), calls=%async_computation.17 | async-start | bytes 12255232 | tf_op jit(solution)/shard_map/psum | solution.py:269
  756.5 4.2 copy-start.22
  756.5 34.0 %copy-start.5 = (f32[128,1024]{1,0:T(8,128)S(1)}, f32[128,1024]{1,0:T(8,128)}, u32[]{:S(2)}) copy-start(f32[128,1024]{1,0:T(8,128)} %copy-done.4) | copy-start | bytes 1572868
  971.2 2.7 copy-start.11
  (10 other events, 14.8 us)
Sparse Core Ops, SparseCore 0:
  9.5 49.0 all-gather.7
  75.9 118.6 all-gather.9
  196.1 21.3 all-gather.11
  219.0 71.6 all-gather.13
  292.1 41.1 all-gather.15
  376.9 68.2 reduce-scatter.18
  448.8 67.6 reduce-scatter.20
  519.0 30.2 reduce-scatter.12
  552.5 52.1 reduce-scatter.16
  607.1 58.8 reduce-scatter.10
  668.6 85.9 reduce-scatter.14
  759.2 207.7 all-reduce.6
